TPU v7x, 32 devices: a whole 2x2x4 slice. The times are simulated.
32 devices in a mesh: fn: 32 (over z, y, x, core).
Axes of the slice: x: 2, y: 2, z: 4, core: 2. Of those that a mesh axis runs over, the one named last changes fastest.
Arguments:
- support_functions: float32 [96, 64, 2048], P('fn'), may hold values from -50 to 50
- owner_counts: int32 [32], replicated, may hold values from 1 to 3, as said below
- region_shift: int32 [96], P('fn'), may hold values from 0 to 63
- kernel: float32 [64, 64], replicated, may hold values from -0.75 to 0.75
- external: float32 [131072], P('fn'), may hold values from -1 to 1
- kinetic_taps: float32 [15], replicated, may hold values from -3 to 3
- magic_taps: float32 [16], replicated, may hold values from -0.6 to 1.6
Outputs:
- filtered: float32 [64, 64, 2048], P('fn')
Inputs may be any that keep to these rules, and one draw needn't show every extreme that they name: `owner_counts`: each owner's number of live slots; owners 2k and 2k+1 together hold exactly 4 live slots, so the counts sum to 64; slots at or past an owner's count hold no function.
All inputs are finite; a program needn't handle non-finite values.
Results may differ from a plain program's by a relative error of at most 0.0003.
Values sent between devices are 32-bit elements; how exact they have to be, the bound alone decides.
A program may use at most 64 MiB of HBM per device.

v0:
```python
import functools

import jax
import jax.numpy as jnp
from jax import lax
from jax.experimental import pallas as pl
from jax.experimental.pallas import tpu as pltpu
from jax.sharding import PartitionSpec as P

NY = 64
NZ = 32
LANES = 128
SLAB = 256
YS = SLAB // NZ
VMEM = pl.BlockSpec(memory_space=pltpu.VMEM)
SMEM = pl.BlockSpec(memory_space=pltpu.SMEM)
F32 = jnp.float32
BF16 = jnp.bfloat16


def halves(values):
    high = values.astype(BF16)
    low = (values - high.astype(F32)).astype(BF16)
    return high, low


def dot(left, right):
    return jnp.dot(left, right, preferred_element_type=F32)


def params(limit=48 << 20):
    return pltpu.CompilerParams(vmem_limit_bytes=limit)


def roll_kernel(rows_per, shift_ref, slots_ref, own_ref, out_ref, flat_ref):
    slot_each, nx, cells = slots_ref.shape
    q_count = cells // LANES
    unit = min(rows_per, q_count)
    total = nx * q_count
    for s in range(slot_each):
        for q in range(q_count):
            flat_ref[s, pl.ds(q, nx, stride=q_count), :] = slots_ref[s, :, q * LANES:(q + 1) * LANES]
    for s in reversed(range(slot_each)):
        back = shift_ref[s] * q_count
        for u in range(total // unit):
            source = lax.rem(u * unit - back + total, total)
            block = flat_ref[s, pl.ds(pl.multiple_of(source, 8), unit), :]
            dest, within = u * unit // rows_per, u * unit % rows_per
            if s == slot_each - 1:
                out_ref[dest, within:within + unit, :] = block
            else:
                own_ref[dest, s * rows_per + within:s * rows_per + within + unit, :] = block


def matrices_kernel(devices, kin_ref, mag_ref, place_ref, kernel_ref, xf_ref, xb_ref, kin_out, fwd_out, bwd_out, mix_out):
    nx = xb_ref.shape[0]
    kin_half = kin_ref.shape[0]
    taps = mag_ref.shape[0]
    kin_count = 2 * kin_half - 1
    kin_center, mag_center = kin_count // 2, taps // 2
    kin = [-0.5 * kin_ref[abs(t - kin_center)] for t in range(kin_count)]
    mag = [mag_ref[t] for t in range(taps)]
    total = functools.reduce(lambda a, b: a + b, [jnp.abs(m) for m in mag])

    def picked(index, values, first=0):
        summed = jnp.zeros(index.shape, F32)
        for t, value in enumerate(values):
            summed = jnp.where(index == t + first, value, summed)
        return summed

    def iota(shape, dim):
        return lax.broadcasted_iota(jnp.int32, shape, dim)

    spread = max(nx // devices, 1)
    def x_of(row):
        if spread == 1:
            return row
        return lax.rem(row, devices) * spread + row // devices

    out_x, in_x = x_of(iota((nx, nx), 0)), x_of(iota((nx, nx), 1))
    ahead = lax.rem(in_x - out_x + mag_center + nx, nx)
    behind = lax.rem(out_x - in_x + mag_center + nx, nx)
    across = lax.rem(in_x - out_x + kin_center + nx, nx)
    fh, fl = halves(picked(ahead, mag) / total)
    kh, kl = halves(picked(across, kin))
    bh, bl = halves(picked(behind, mag) / total)
    xf_ref[:nx] = jnp.concatenate([fh, fl, fh], axis=1)
    xf_ref[nx:] = jnp.concatenate([kh, kl, kh], axis=1)
    xb_ref[...] = jnp.concatenate([bh, bl, bh], axis=1)

    square = (SLAB, SLAB)
    row, col = iota(square, 0), iota(square, 1)
    in_y, in_z = row // NZ, lax.rem(row, NZ)
    out_y, out_z = col // NZ, lax.rem(col, NZ)
    dy, dz = in_y - out_y, in_z - out_z

    def along_y(delta, values, center, d):
        low = max(YS * d + center - (YS - 1), 0)
        high = min(YS * d + center + YS - 1, len(values) - 1)
        return picked(delta + (YS * d + center), values[low:high + 1], low)

    mag_z = picked(lax.rem(dz + mag_center + NZ, NZ), mag) / total
    mag_zt = picked(lax.rem(mag_center - dz + NZ, NZ), mag) / total
    kin_z = picked(lax.rem(dz + kin_center + NZ, NZ), kin)
    reach = fwd_out.shape[0] // 2 // SLAB // 2
    kin_reach = kin_out.shape[0] // 2 // SLAB // 2
    for n in range(2 * reach + 1):
        d = n - reach
        for out, y_part, z_part in (
            (fwd_out, along_y(dy, mag, mag_center, d), mag_z),
            (bwd_out, along_y(-dy, mag, mag_center, -d), mag_zt),
        ):
            high, low = halves(y_part / total * z_part)
            out[n * SLAB:(n + 1) * SLAB] = high
            base = (2 * reach + 1 + n) * SLAB
            out[base:base + SLAB] = low
    for n in range(2 * kin_reach + 1):
        d = n - kin_reach
        value = jnp.where(dz == 0, along_y(dy, kin, kin_center, d), 0.0)
        if d == 0:
            value = value + jnp.where(dy == 0, kin_z, 0.0)
        high, low = halves(value)
        kin_out[n * SLAB:(n + 1) * SLAB] = high
        base = (2 * kin_reach + 1 + n) * SLAB
        kin_out[base:base + SLAB] = low

    functions = kernel_ref.shape[0]
    local = functions // devices
    full = (functions, functions)
    wanted = lax.rem(iota(full, 0), devices) * local + iota(full, 0) // devices
    row_pick = jnp.where(wanted == iota(full, 1), 1.0, 0.0).astype(BF16)
    col_pick = jnp.where(iota(full, 0) == place_ref[...], 1.0, 0.0).astype(BF16)
    parts = [dot(dot(row_pick, part).astype(BF16), col_pick).astype(BF16) for part in halves(kernel_ref[...])]
    mix_out[...] = jnp.concatenate([parts[0], parts[1], parts[0]], axis=1)


def mix_kernel(devices, arrived_ref, mix_ref, external_ref, out_ref, up_ref, down_ref):
    functions = mix_ref.shape[0]
    local = functions // devices
    rows_per = external_ref.shape[0]
    stride = out_ref.shape[0] // devices
    half = devices // 2
    count = functions // 2
    for c in range(0, rows_per, 2):
        values = jnp.concatenate(
            [arrived_ref[pl.ds(c + k, functions, stride=rows_per), :] for k in range(2)], axis=1
        )
        high, low = halves(values)
        mixed = dot(mix_ref[...], jnp.concatenate([high, high, low], axis=0))
        up = down = 0.0
        for j in range(local):
            part = mixed[j * devices:(j + 1) * devices]
            for k in range(2):
                out_ref[pl.ds(j * rows_per + c + k, devices, stride=stride), :] = part[:, k * LANES:(k + 1) * LANES]
            squared = part * part
            up = up + jnp.sum(squared[:half], axis=0, keepdims=True)
            down = down + jnp.sum(squared[half:], axis=0, keepdims=True)
        for k in range(2):
            up_ref[c + k:c + k + 1, :] = up[:, k * LANES:(k + 1) * LANES]
            down_ref[c + k:c + k + 1, :] = down[:, k * LANES:(k + 1) * LANES]

    def cube_root(x):
        guess = jnp.exp(jnp.log(x) * (1.0 / 3.0))
        return guess - (guess - x / (guess * guess)) * (1.0 / 3.0)

    rho_up, rho_down = up_ref[...] / count, down_ref[...] / count
    shared = external_ref[...] + 0.5 * (rho_up + rho_down)
    spins = [shared - cube_root((6.0 / jnp.pi) * rho + 1e-6) for rho in (rho_up, rho_down)]
    peak = jnp.maximum(jnp.max(jnp.abs(spins[0])), jnp.max(jnp.abs(spins[1])))
    tail = jnp.full((8, LANES), peak, F32)
    for dest in range(devices):
        base = dest * stride + local * rows_per
        out_ref[base:base + rows_per, :] = spins[dest // half]
        out_ref[base + rows_per:base + rows_per + 8, :] = tail


def filter_kernel(devices, rows_per, kin_ref, got_ref, xf_ref, xb_ref, kinm_ref, fwd_ref, bwd_ref, out_ref,
                  v_hi, v_lo, p_hi, p_lo, w_hi, w_lo, acc_ref, pot_ref, stage_ref):
    local, nx, cells = out_ref.shape
    slabs = cells // SLAB
    q_count = cells // LANES
    per_slab = SLAB // LANES
    stride = got_ref.shape[0] // devices
    spread = max(rows_per // q_count, 1)

    def plane(field, q):
        if rows_per >= q_count:
            return jnp.concatenate([
                got_ref[pl.ds(field * rows_per + xo * q_count + q, devices, stride=stride), :]
                for xo in range(spread)
            ], axis=0)
        split = q_count // rows_per
        start = (q // rows_per) * stride + field * rows_per + q % rows_per
        return got_ref[pl.ds(start, nx, stride=split * stride), :]

    def slab_of(field, h):
        return jnp.concatenate([plane(field, h * per_slab + k) for k in range(per_slab)], axis=1)

    for h in range(slabs):
        pot_ref[h] = slab_of(local, h)
        for f in range(local):
            high, low = halves(slab_of(f, h))
            where = slice(f * nx, (f + 1) * nx)
            v_hi[h, where] = high
            v_lo[h, where] = low
            both = dot(xf_ref[...], jnp.concatenate([high, high, low], axis=0))
            p_hi[h, where], p_lo[h, where] = halves(both[:nx])
            acc_ref[h, where] = both[nx:]

    def banded(hi_ref, lo_ref, matrix_ref, h):
        width = matrix_ref.shape[0] // 2
        count = width // SLAB
        places = [lax.rem(h + (n - count // 2) + slabs, slabs) for n in range(count)]
        high = jnp.concatenate([hi_ref[place] for place in places], axis=1)
        low = jnp.concatenate([lo_ref[place] for place in places], axis=1)
        return dot(high, matrix_ref[:width]) + (dot(low, matrix_ref[:width]) + dot(high, matrix_ref[width:]))

    def forward(h, carry):
        acc_ref[h] += banded(v_hi, v_lo, kinm_ref, h)
        smooth = banded(p_hi, p_lo, fwd_ref, h)
        potential = pot_ref[h]
        for f in range(local):
            high, low = halves(smooth[f * nx:(f + 1) * nx] * potential)
            mixed = dot(xb_ref[...], jnp.concatenate([high, high, low], axis=0))
            w_hi[h, f * nx:(f + 1) * nx], w_lo[h, f * nx:(f + 1) * nx] = halves(mixed)
        return carry

    lax.fori_loop(0, slabs, forward, 0)

    sides = jnp.abs(kin_ref[0])
    for t in range(1, kin_ref.shape[0]):
        sides = sides + 2.0 * jnp.abs(kin_ref[t])
    peaks = got_ref[pl.ds((local + 1) * rows_per, devices, stride=stride), :]
    bound = 1.0 + 1.5 * sides + jnp.max(peaks, axis=0, keepdims=True)
    bound = jnp.concatenate([bound] * per_slab, axis=1)

    def backward(h, carry):
        result = (acc_ref[h] + banded(w_hi, w_lo, bwd_ref, h)) / bound
        lanes = pl.multiple_of(h * SLAB, SLAB)
        for f in range(local):
            for xo in range(spread):
                count = nx // spread
                block = result[f * nx + xo * count:f * nx + (xo + 1) * count]
                for k in range(per_slab):
                    stage_ref[f, h * per_slab + k, pl.ds(xo, count, stride=spread), :] = block[:, k * LANES:(k + 1) * LANES]
        for f in range(local):
            for k in range(per_slab):
                out_ref[f, :, pl.ds(pl.multiple_of(lanes + k * LANES, LANES), LANES)] = stage_ref[f, h * per_slab + k]
        return carry

    lax.fori_loop(0, slabs, backward, 0)


def shaped(shape, dtype=F32):
    return jax.ShapeDtypeStruct(shape, dtype)


def body(support_functions, owner_counts, region_shift, kernel, external, kinetic_taps, magic_taps):
    devices = lax.axis_size("fn")
    position = lax.axis_index("fn")
    slot_each, nx, cells = support_functions.shape
    functions = kernel.shape[0]
    local = functions // devices
    rows_per = nx * cells // devices // LANES
    reach = -(-(magic_taps.shape[0] // 2) // YS)
    kin_reach = -(-(kinetic_taps.shape[0] - 1) // YS)

    own, outgoing = pl.pallas_call(
        functools.partial(roll_kernel, rows_per),
        out_shape=(shaped((devices, local * rows_per, LANES)), shaped((devices, rows_per, LANES))),
        in_specs=[SMEM, VMEM],
        out_specs=(VMEM, VMEM),
        scratch_shapes=[pltpu.VMEM((slot_each, nx * cells // LANES, LANES), F32)],
        compiler_params=params(),
        name="roll",
    )(region_shift, support_functions)

    route = [(d, d ^ 1) for d in range(devices)]
    received = lax.ppermute(outgoing, "fn", route)
    lone = owner_counts[position] < local
    balanced = own.at[:, rows_per:].set(jnp.where(lone, received, own[:, rows_per:]))
    arrived = lax.all_to_all(balanced, "fn", split_axis=0, concat_axis=0, tiled=True)

    pairs = jnp.arange(devices // 2, dtype=jnp.int32)[:, None] * (2 * local)
    counts = owner_counts.reshape(-1, 2)
    first = pairs + jnp.concatenate([jnp.zeros_like(counts[:, :1]), counts[:, :1]], axis=1)
    stand_in = pairs + jnp.asarray([[2 * local - 1, local]], jnp.int32)
    second = jnp.where(counts < local, stand_in, first + 1)
    places = jnp.stack([first, second], axis=-1).reshape(1, functions)

    xf, xb, kin_m, fwd_m, bwd_m, mix_m = pl.pallas_call(
        functools.partial(matrices_kernel, devices),
        out_shape=(
            shaped((2 * nx, 3 * nx), BF16),
            shaped((nx, 3 * nx), BF16),
            shaped((2 * (2 * kin_reach + 1) * SLAB, SLAB), BF16),
            shaped((2 * (2 * reach + 1) * SLAB, SLAB), BF16),
            shaped((2 * (2 * reach + 1) * SLAB, SLAB), BF16),
            shaped((functions, 3 * functions), BF16),
        ),
        in_specs=[SMEM, SMEM, VMEM, VMEM],
        out_specs=(VMEM,) * 6,
        compiler_params=params(),
        cost_estimate=pl.CostEstimate(flops=1 << 27, bytes_accessed=4 << 20, transcendentals=0),
        name="matrices",
    )(kinetic_taps, magic_taps, places, kernel)

    stride = (local + 1) * rows_per + 8
    payload = pl.pallas_call(
        functools.partial(mix_kernel, devices),
        out_shape=shaped((devices * stride, LANES)),
        in_specs=[VMEM, VMEM, VMEM],
        out_specs=VMEM,
        scratch_shapes=[pltpu.VMEM((rows_per, LANES), F32)] * 2,
        compiler_params=params(),
        name="mix",
    )(arrived.reshape(-1, LANES), mix_m, external.reshape(rows_per, LANES))

    got = lax.all_to_all(payload.reshape(devices, stride, LANES), "fn", split_axis=0, concat_axis=0, tiled=True)

    slabs = cells // SLAB
    tile = (slabs, local * nx, SLAB)
    return pl.pallas_call(
        functools.partial(filter_kernel, devices, rows_per),
        out_shape=shaped((local, nx, cells)),
        in_specs=[SMEM] + [VMEM] * 6,
        out_specs=VMEM,
        scratch_shapes=[pltpu.VMEM(tile, BF16)] * 6
        + [pltpu.VMEM(tile, F32), pltpu.VMEM((slabs, nx, SLAB), F32),
           pltpu.VMEM((local, cells // LANES, nx, LANES), F32)],
        compiler_params=params(),
        name="filter",
    )(kinetic_taps, got.reshape(-1, LANES), xf, xb, kin_m, fwd_m, bwd_m)


def solution(mesh):
    placed = (P("fn", None, None), P(), P("fn"), P(), P("fn"), P(), P())
    return jax.shard_map(
        body, mesh=mesh, in_specs=placed, out_specs=P("fn", None, None), check_vma=False
    )
```

profile of v0, /device:TPU:0, one launch (start us, length us, event | category | flops | bytes accessed | tf_op | source)
XLA Modules:
  0.0 97.9 jit_solution(3049627921446124729)
XLA Ops:
  0.0 1.4 %copy-done = f32[3,64,2048]{2,1,0:T(8,128)S(1)} copy-done((f32[3,64,2048]{2,1,0:T(8,128)S(1)}, f32[3,64,2048]{2,1,0:T(8,128)}, u32[]{:S(2)}) %copy-start) | copy-done | bytes 1572888
  1.4 0.7 copy-done.4
  2.1 2.6 %roll.1 = (f32[32,64,128]{2,1,0:T(8,128)}, f32[32,32,128]{2,1,0:T(8,128)S(1)}) custom-call(s32[3]{0:T(128)S(1)} %copy-done.4, f32[3,64,2048]{2,1,0:T(8,128)S(1)} %copy-done), custom_call_target="tpu_custom_call" | custom-call | tf_op jit(solution)/shard_map/roll/pallas_call | solution.py:268
  4.7 0.5 collective-permute-start
  5.2 1.3 %dynamic_slice.3 = s32[1]{0:T(128)} dynamic-slice(s32[32]{0:T(128)} %param.11, s32[]{:T(128)S(6)} %select_n.15), dynamic_slice_sizes={1} | dynamic-slice | bytes 12 | tf_op jit(solution)/shard_map/dynamic_slice | solution.py:280
  7.1 0.0 collective-permute-done
  7.1 0.0 copy-start.9
  7.1 0.0 copy-start.8
  7.2 0.0 copy-start.5
  7.2 0.0 copy-start.6
  7.2 0.0 copy-start.7
  7.2 1.9 %select_dynamic-update-slice_fusion = f32[32,64,128]{2,1,0:T(8,128)} fusion(f32[32,64,128]{2,1,0:T(8,128)} %get-tuple-element.25, f32[32,32,128]{2,1,0:T(8,128)S(1)} %collective-permute-done, pred[]{:T(512)} %bitcast), kind=kLoop, calls=%fused_computation | loop fusion | flops 131072 | bytes 1573376 | tf_op jit(solution)/shard_map/scatter | solution.py:281
  9.1 7.0 %all-to-all-start = ((f32[32,64,128]{2,1,0:T(8,128)}), f32[32,64,128]{2,1,0:T(8,128)S(1)}, u32[]{:S(2)}, u32[]{:S(2)}) async-start(f32[32,64,128]{2,1,0:T(8,128)} %select_dynamic-update-slice_fusion), calls=%async_computation | async-start | bytes 2097152 | tf_op jit(solution)/shard_map/all_to_all | solution.py:282
  16.1 0.0 copy-done.9
  16.1 0.1 reshape.57
  16.2 0.0 copy-done.8
  16.2 0.1 pad_add_fusion
  16.3 0.1 copy.12
  16.4 0.1 copy.13
  16.4 0.1 copy.14
  16.5 0.1 reshape.58.place_ref
  16.7 0.0 copy-done.5
  16.7 0.0 copy-done.6
  16.7 0.0 copy-done.7
  16.7 8.3 %matrices.1 = (bf16[128,192]{1,0:T(8,128)(2,1)S(1)}, bf16[64,192]{1,0:T(8,128)(2,1)S(1)}, bf16[2560,256]{1,0:T(8,128)(2,1)S(1)}, bf16[1536,256]{1,0:T(8,128)(2,1...) custom-call(f32[15]{0:T(128)S(1)} %copy-done.5, f32[16]{0:T(128)S(1)} %copy-done.7, ...), custom_call_target="tpu_custom_call" | custom-call | flops 134217728 | bytes 4194304 | tf_op jit(solution)/shard_map/matrices/pallas_call | solution.py:291
  25.0 0.9 copy-done.1
  25.9 16.4 %all-to-all-done = f32[32,64,128]{2,1,0:T(8,128)S(1)} async-done(((f32[32,64,128]{2,1,0:T(8,128)}), f32[32,64,128]{2,1,0:T(8,128)S(1)}, u32[]{:S(2)}, u32[]{:S(2)}) %all-to-all-start) | async-done | bytes 1048608 | tf_op jit(solution)/shard_map/all_to_all | solution.py:282
  42.3 0.0 copy-done.3
  42.3 1.1 %mix.1 = f32[3328,128]{1,0:T(8,128)S(1)} custom-call(f32[2048,128]{1,0:T(8,128)S(1)} %bitcast.10, bf16[64,192]{1,0:T(8,128)(2,1)S(1)} %get-tuple-element.27.mix_ref, f32[32,128]{1,0:T(8,128)S(1)} %bitcast.11), custom_call_target="tpu_custom_call" | custom-call | tf_op jit(solution)/shard_map/mix/pallas_call | solution.py:309
  43.4 0.0 copy-start.2
  43.4 43.9 %all_to_all.10 = f32[32,104,128]{2,1,0:T(8,128)S(1)} all-to-all(f32[32,104,128]{2,1,0:T(8,128)S(1)} %bitcast.9), channel_id=1, replica_groups=mesh['fn'=32] {'fn'}, dimensions={0} | all-to-all | bytes 3407872 | tf_op jit(solution)/shard_map/all_to_all | solution.py:319
  87.3 10.6 %filter.1 = f32[2,64,2048]{2,1,0:T(8,128)} custom-call(f32[15]{0:T(128)S(1)} %copy-done.5, f32[3328,128]{1,0:T(8,128)S(1)} %bitcast.8, bf16[128,192]{1,0:T(8,128)(2,1)S(1)} %get-tuple-element.28.xf_ref, bf16[64,192]{1,0:T(8,128)(2,1)S(1)} %get-tuple-element.29.xb_ref, bf16[2560,256]{1,0:T(8,128)(2,1)S(1)} %get-tuple-element.30.kinm_ref, ...), custom_call_target="tpu_custom_call" | custom-call | tf_op jit(solution)/shard_map/filter/pallas_call | solution.py:323
  (7 shorter events, 0.0 us)
Async XLA Ops:
  0.0 1.4 %copy-start = (f32[3,64,2048]{2,1,0:T(8,128)S(1)}, f32[3,64,2048]{2,1,0:T(8,128)}, u32[]{:S(2)}) copy-start(f32[3,64,2048]{2,1,0:T(8,128)} %slots_ref.1) | copy-start | bytes 4718596
  1.4 0.7 copy-start.4
  4.7 2.4 %collective-permute-start = (f32[32,32,128]{2,1,0:T(8,128)S(1)}, f32[32,32,128]{2,1,0:T(8,128)S(1)}, u32[]{:S(2)}, u32[]{:S(2)}) collective-permute-start(f32[32,32,128]{2,1,0:T(8,128)S(1)} %get-tuple-element.26), channel_id=1, source_target_pairs={{0,1},{1,0},{2,3},{3,2},{4,5},{5,4},{6,7},{7,6},{8,9},{9,8},{10,11... | collective-permute-start | bytes 1572872 | tf_op jit(solution)/shard_map/ppermute | solution.py:279
  7.1 9.0 %copy-start.9 = (s32[32]{0:T(128)S(1)}, s32[32]{0:T(128)}, u32[]{:S(2)}) copy-start(s32[32]{0:T(128)} %param.11) | copy-start | bytes 388
  7.1 9.1 %copy-start.8 = (s32[2]{0:T(128)S(1)}, s32[2]{0:T(128)}, u32[]{:S(2)}) copy-start(s32[2]{0:T(128)} %constant.52) | copy-start | bytes 28
  7.2 9.5 %copy-start.5 = (f32[15]{0:T(128)S(1)}, f32[15]{0:T(128)}, u32[]{:S(2)}) copy-start(f32[15]{0:T(128)} %kin_ref.3) | copy-start | bytes 184
  7.2 9.5 %copy-start.6 = (f32[64,64]{1,0:T(8,128)S(1)}, f32[64,64]{1,0:T(8,128)}, u32[]{:S(2)}) copy-start(f32[64,64]{1,0:T(8,128)} %kernel_ref.1) | copy-start | bytes 49156
  7.2 9.5 %copy-start.7 = (f32[16]{0:T(128)S(1)}, f32[16]{0:T(128)}, u32[]{:S(2)}) copy-start(f32[16]{0:T(128)} %mag_ref.1) | copy-start | bytes 196
  9.1 33.2 %copy-start.3 = (f32[4096]{0:T(1024)S(1)}, f32[4096]{0:T(1024)}, u32[]{:S(2)}) copy-start(f32[4096]{0:T(1024)} %param.14) | copy-start | bytes 49156
  9.1 33.2 %all-to-all-start = ((f32[32,64,128]{2,1,0:T(8,128)}), f32[32,64,128]{2,1,0:T(8,128)S(1)}, u32[]{:S(2)}, u32[]{:S(2)}) async-start(f32[32,64,128]{2,1,0:T(8,128)} %select_dynamic-update-slice_fusion), calls=%async_computation | async-start | bytes 2097152 | tf_op jit(solution)/shard_map/all_to_all | solution.py:282
  25.0 0.9 copy-start.1
  43.4 43.9 %copy-start.2 = (bf16[1536,256]{1,0:T(8,128)(2,1)S(1)}, bf16[1536,256]{1,0:T(8,128)(2,1)}, u32[]{:S(2)}) copy-start(bf16[1536,256]{1,0:T(8,128)(2,1)} %copy-done.1) | copy-start | bytes 2359300
where the time goes:
time: 98.3 us; the launch traced here: 97.9 us
  blocking collectives  43.9 us (45%)
  Pallas kernels  22.6 us (23%)
  waiting for transfers between devices  16.4 us (17%)
  starting transfers between devices  7.44 us (8%)
  local copies, waits for them, and re-layouts  4.77 us (5%)
  other arithmetic  2.02 us (2%)
    all_to_all x1, blocking collectives, body(): lax.all_to_all(payload.reshape(devices, stride, LANES), 'fn', split_axis=...  43.9 us
    all_to_all x1, waiting for transfers between devices, body(): lax.all_to_all(balanced, 'fn', split_axis=0, concat_axis=0, tiled=True)  16.4 us
    pallas_call x1, Pallas kernels, body(): pl.pallas_call(functools.partial(filter_kernel, devices, rows_per), out_s...  10.6 us
    pallas_call x1, Pallas kernels, body(): pl.pallas_call(functools.partial(matrices_kernel, devices), out_shape=(sh...  8.26 us
    all_to_all x1, starting transfers between devices, body(): lax.all_to_all(balanced, 'fn', split_axis=0, concat_axis=0, tiled=True)  6.95 us
    unnamed x20, local copies, waits for them, and re-layouts  3.01 us
    pallas_call x1, Pallas kernels, body(): pl.pallas_call(functools.partial(roll_kernel, rows_per), out_shape=(shape...  2.64 us
  transfers between devices with their start and end apart: 2, of which 1 were waited for; matrix products, arithmetic and copies ran while one was open for 2% of the time, Pallas kernels for 8%

commit v1 on v0

--- a/solution.py
+++ b/solution.py
@@ -28,8 +28,8 @@
     return jnp.dot(left, right, preferred_element_type=F32)
 
 
-def params(limit=48 << 20):
-    return pltpu.CompilerParams(vmem_limit_bytes=limit)
+def params(**more):
+    return pltpu.CompilerParams(vmem_limit_bytes=48 << 20, has_side_effects="collective_id" in more, **more)
 
 
 def roll_kernel(rows_per, shift_ref, slots_ref, own_ref, out_ref, flat_ref):
@@ -134,7 +134,85 @@
     mix_out[...] = jnp.concatenate([parts[0], parts[1], parts[0]], axis=1)
 
 
-def mix_kernel(devices, arrived_ref, mix_ref, external_ref, out_ref, up_ref, down_ref):
+def partner(me, k):
+    bit = 1
+    there = me
+    while bit <= k:
+        if k & bit:
+            there = there + bit - 2 * bit * ((me // bit) % 2)
+        bit *= 2
+    return there
+
+
+def far_first(devices):
+    half = devices // 2
+    order = []
+    for n in range(half):
+        order += [half + n, n]
+    return [k for k in order if k]
+
+
+def greet(me, devices):
+    barrier = pltpu.get_barrier_semaphore()
+    for k in range(1, devices):
+        pl.semaphore_signal(barrier, inc=1, device_id=(partner(me, k),), device_id_type=pl.DeviceIdType.MESH)
+    pl.semaphore_wait(barrier, devices - 1)
+
+
+def remote(source, target, send, recv, device):
+    return pltpu.make_async_remote_copy(
+        src_ref=source, dst_ref=target, send_sem=send, recv_sem=recv,
+        device_id=(device,), device_id_type=pl.DeviceIdType.MESH,
+    )
+
+
+def scatter_kernel(devices, kin_ref, mag_ref, place_ref, kernel_ref, own_ref,
+                   xf_ref, xb_ref, kin_out, fwd_out, bwd_out, mix_out, got_ref, send_sem, recv_sem):
+    me = lax.axis_index("fn")
+    greet(me, devices)
+    copies = []
+    for k in far_first(devices):
+        there = partner(me, k)
+        copy = remote(own_ref.at[there], got_ref.at[me], send_sem.at[k], recv_sem.at[k], there)
+        copy.start()
+        copies.append(copy)
+    got_ref[me] = own_ref[me]
+    matrices_kernel(devices, kin_ref, mag_ref, place_ref, kernel_ref, xf_ref, xb_ref, kin_out, fwd_out, bwd_out, mix_out)
+    for copy in copies:
+        copy.wait()
+
+
+def return_kernel(devices, mixed_ref, pots_ref, got_ref, gpot_ref, send_sem, recv_sem, own_send, own_recv, relay_send, relay_recv):
+    me = lax.axis_index("fn")
+    half = devices // 2
+    side = me // half
+    across = partner(me, half)
+    greet(me, devices)
+    handed = remote(pots_ref.at[1 - side], gpot_ref.at[me], own_send.at[0], own_recv.at[0], across)
+    handed.start()
+    copies = []
+    for k in range(1, half):
+        copy = remote(pots_ref.at[side], gpot_ref.at[me], own_send.at[k], own_recv.at[k], partner(me, k))
+        copy.start()
+        copies.append(copy)
+    order = far_first(devices)
+    for n, k in enumerate(order):
+        there = partner(me, k)
+        copy = remote(mixed_ref.at[there], got_ref.at[me], send_sem.at[k], recv_sem.at[k], there)
+        copy.start()
+        copies.append(copy)
+    got_ref[me] = mixed_ref[me]
+    gpot_ref[me] = pots_ref[side]
+    handed.wait()
+    for k in range(1, half):
+        copy = remote(gpot_ref.at[across], gpot_ref.at[across], relay_send.at[k], relay_recv.at[k], partner(me, k))
+        copy.start()
+        copies.append(copy)
+    for copy in copies:
+        copy.wait()
+
+
+def mix_kernel(devices, arrived_ref, mix_ref, external_ref, out_ref, pots_ref, up_ref, down_ref):
     functions = mix_ref.shape[0]
     local = functions // devices
     rows_per = external_ref.shape[0]
@@ -168,30 +246,29 @@
     spins = [shared - cube_root((6.0 / jnp.pi) * rho + 1e-6) for rho in (rho_up, rho_down)]
     peak = jnp.maximum(jnp.max(jnp.abs(spins[0])), jnp.max(jnp.abs(spins[1])))
     tail = jnp.full((8, LANES), peak, F32)
-    for dest in range(devices):
-        base = dest * stride + local * rows_per
-        out_ref[base:base + rows_per, :] = spins[dest // half]
-        out_ref[base + rows_per:base + rows_per + 8, :] = tail
-
-
-def filter_kernel(devices, rows_per, kin_ref, got_ref, xf_ref, xb_ref, kinm_ref, fwd_ref, bwd_ref, out_ref,
+    for spin in range(2):
+        pots_ref[spin, :rows_per] = spins[spin]
+        pots_ref[spin, rows_per:] = tail
+
+
+def filter_kernel(devices, rows_per, kin_ref, got_ref, gpot_ref, xf_ref, xb_ref, kinm_ref, fwd_ref, bwd_ref, out_ref,
                   v_hi, v_lo, p_hi, p_lo, w_hi, w_lo, acc_ref, pot_ref, stage_ref):
     local, nx, cells = out_ref.shape
     slabs = cells // SLAB
     q_count = cells // LANES
     per_slab = SLAB // LANES
-    stride = got_ref.shape[0] // devices
     spread = max(rows_per // q_count, 1)
 
     def plane(field, q):
+        ref, first = (gpot_ref, 0) if field == local else (got_ref, field * rows_per)
+        stride = ref.shape[0] // devices
         if rows_per >= q_count:
             return jnp.concatenate([
-                got_ref[pl.ds(field * rows_per + xo * q_count + q, devices, stride=stride), :]
-                for xo in range(spread)
+                ref[pl.ds(first + xo * q_count + q, devices, stride=stride), :] for xo in range(spread)
             ], axis=0)
         split = q_count // rows_per
-        start = (q // rows_per) * stride + field * rows_per + q % rows_per
-        return got_ref[pl.ds(start, nx, stride=split * stride), :]
+        start = (q // rows_per) * stride + first + q % rows_per
+        return ref[pl.ds(start, nx, stride=split * stride), :]
 
     def slab_of(field, h):
         return jnp.concatenate([plane(field, h * per_slab + k) for k in range(per_slab)], axis=1)
@@ -230,7 +307,7 @@
     sides = jnp.abs(kin_ref[0])
     for t in range(1, kin_ref.shape[0]):
         sides = sides + 2.0 * jnp.abs(kin_ref[t])
-    peaks = got_ref[pl.ds((local + 1) * rows_per, devices, stride=stride), :]
+    peaks = gpot_ref[pl.ds(rows_per, devices, stride=gpot_ref.shape[0] // devices), :]
     bound = 1.0 + 1.5 * sides + jnp.max(peaks, axis=0, keepdims=True)
     bound = jnp.concatenate([bound] * per_slab, axis=1)
 
@@ -279,7 +356,6 @@
     received = lax.ppermute(outgoing, "fn", route)
     lone = owner_counts[position] < local
     balanced = own.at[:, rows_per:].set(jnp.where(lone, received, own[:, rows_per:]))
-    arrived = lax.all_to_all(balanced, "fn", split_axis=0, concat_axis=0, tiled=True)
 
     pairs = jnp.arange(devices // 2, dtype=jnp.int32)[:, None] * (2 * local)
     counts = owner_counts.reshape(-1, 2)
@@ -288,8 +364,9 @@
     second = jnp.where(counts < local, stand_in, first + 1)
     places = jnp.stack([first, second], axis=-1).reshape(1, functions)
 
-    xf, xb, kin_m, fwd_m, bwd_m, mix_m = pl.pallas_call(
-        functools.partial(matrices_kernel, devices),
+    each = pltpu.SemaphoreType.DMA((devices,))
+    xf, xb, kin_m, fwd_m, bwd_m, mix_m, arrived = pl.pallas_call(
+        functools.partial(scatter_kernel, devices),
         out_shape=(
             shaped((2 * nx, 3 * nx), BF16),
             shaped((nx, 3 * nx), BF16),
@@ -297,40 +374,48 @@
             shaped((2 * (2 * reach + 1) * SLAB, SLAB), BF16),
             shaped((2 * (2 * reach + 1) * SLAB, SLAB), BF16),
             shaped((functions, 3 * functions), BF16),
+            shaped((devices, local * rows_per, LANES)),
         ),
-        in_specs=[SMEM, SMEM, VMEM, VMEM],
-        out_specs=(VMEM,) * 6,
-        compiler_params=params(),
-        cost_estimate=pl.CostEstimate(flops=1 << 27, bytes_accessed=4 << 20, transcendentals=0),
-        name="matrices",
-    )(kinetic_taps, magic_taps, places, kernel)
-
-    stride = (local + 1) * rows_per + 8
-    payload = pl.pallas_call(
+        in_specs=[SMEM, SMEM, VMEM, VMEM, VMEM],
+        out_specs=(VMEM,) * 7,
+        scratch_shapes=[each, each],
+        compiler_params=params(collective_id=0),
+        name="scatter",
+    )(kinetic_taps, magic_taps, places, kernel, balanced)
+
+    mixed, pots = pl.pallas_call(
         functools.partial(mix_kernel, devices),
-        out_shape=shaped((devices * stride, LANES)),
+        out_shape=(shaped((devices * local * rows_per, LANES)), shaped((2, rows_per + 8, LANES))),
         in_specs=[VMEM, VMEM, VMEM],
-        out_specs=VMEM,
+        out_specs=(VMEM, VMEM),
         scratch_shapes=[pltpu.VMEM((rows_per, LANES), F32)] * 2,
         compiler_params=params(),
         name="mix",
     )(arrived.reshape(-1, LANES), mix_m, external.reshape(rows_per, LANES))
 
-    got = lax.all_to_all(payload.reshape(devices, stride, LANES), "fn", split_axis=0, concat_axis=0, tiled=True)
+    got, gpot = pl.pallas_call(
+        functools.partial(return_kernel, devices),
+        out_shape=(shaped((devices, local * rows_per, LANES)), shaped((devices, rows_per + 8, LANES))),
+        in_specs=[VMEM, VMEM],
+        out_specs=(VMEM, VMEM),
+        scratch_shapes=[each] * 6,
+        compiler_params=params(collective_id=1),
+        name="give_back",
+    )(mixed.reshape(devices, local * rows_per, LANES), pots)
 
     slabs = cells // SLAB
     tile = (slabs, local * nx, SLAB)
     return pl.pallas_call(
         functools.partial(filter_kernel, devices, rows_per),
         out_shape=shaped((local, nx, cells)),
-        in_specs=[SMEM] + [VMEM] * 6,
+        in_specs=[SMEM] + [VMEM] * 7,
         out_specs=VMEM,
         scratch_shapes=[pltpu.VMEM(tile, BF16)] * 6
         + [pltpu.VMEM(tile, F32), pltpu.VMEM((slabs, nx, SLAB), F32),
            pltpu.VMEM((local, cells // LANES, nx, LANES), F32)],
         compiler_params=params(),
         name="filter",
-    )(kinetic_taps, got.reshape(-1, LANES), xf, xb, kin_m, fwd_m, bwd_m)
+    )(kinetic_taps, got.reshape(-1, LANES), gpot.reshape(-1, LANES), xf, xb, kin_m, fwd_m, bwd_m)
 
 
 def solution(mesh):

time: 98.3 us -> 81.9 us (0.83)
  Pallas kernels: 22.6 us -> 77.1 us
  blocking collectives: 43.9 us -> 0 us
  waiting for transfers between devices: 16.4 us -> 0.01 us
  starting transfers between devices: 7.44 us -> 0.56 us
  other arithmetic: 2.02 us -> 0.23 us
  local copies, waits for them, and re-layouts: 4.77 us -> 3.15 us
    pallas_call x2 -> x3, Pallas kernels: 9.36 us -> 63.8 us  [the longest x1 36.1 us: body(): pl.pallas_call(functools.partial(return_kernel, devices), out_shape=(shap...]
    all_to_all x1 -> x0, blocking collectives: 43.9 us -> none  [body(): lax.all_to_all(payload.reshape(devices, stride, LANES), 'fn', split_axis=...]
    all_to_all x1 -> x0, waiting for transfers between devices: 16.4 us -> none  [body(): lax.all_to_all(balanced, 'fn', split_axis=0, concat_axis=0, tiled=True)]
    all_to_all x1 -> x0, starting transfers between devices: 6.95 us -> none  [body(): lax.all_to_all(balanced, 'fn', split_axis=0, concat_axis=0, tiled=True)]
    scatter x1, other arithmetic: 1.94 us -> 0.15 us  [body(): own.at[:, rows_per:].set(jnp.where(lone, received, own[:, rows_per:]))]
    unnamed x20 -> x16, local copies, waits for them, and re-layouts: 3.01 us -> 2.1 us
  transfers between devices with their start and end apart: 2 -> 1, of which waited for: 1 -> 0; matrix products, arithmetic and copies ran while one was open for 2% -> 1% of each run, Pallas kernels for 8% -> 0%
where the time goes in v1:
time: 81.9 us; the launch traced here: 81.8 us
  Pallas kernels  77.1 us (94%)
  local copies, waits for them, and re-layouts  3.15 us (4%)
    pallas_call x1, Pallas kernels, body(): pl.pallas_call(functools.partial(return_kernel, devices), out_shape=(shap...  36.1 us
    pallas_call x1, Pallas kernels, body(): pl.pallas_call(functools.partial(scatter_kernel, devices), out_shape=(sha...  26.2 us
    pallas_call x1, Pallas kernels, body(): pl.pallas_call(functools.partial(filter_kernel, devices, rows_per), out_s...  11.6 us
    unnamed x16, local copies, waits for them, and re-layouts  2.1 us
    pallas_call x1, Pallas kernels, body(): pl.pallas_call(functools.partial(roll_kernel, rows_per), out_shape=(shape...  1.67 us
  transfers between devices with their start and end apart: 1, of which 0 were waited for; matrix products, arithmetic and copies ran while one was open for 1% of the time, Pallas kernels for 0%

profile of v1, /device:TPU:0, one launch (start us, length us, event | category | flops | bytes accessed | tf_op | source)
XLA Modules:
  0.0 81.8 jit_solution(16101456007767946644)
XLA Ops:
  0.0 0.0 copy-start.6
  0.0 0.0 copy-start
  0.0 1.4 %copy-done = f32[3,64,2048]{2,1,0:T(8,128)S(1)} copy-done((f32[3,64,2048]{2,1,0:T(8,128)S(1)}, f32[3,64,2048]{2,1,0:T(8,128)}, u32[]{:S(2)}) %copy-start) | copy-done | bytes 1572888
  1.4 0.0 copy-start.4
  1.4 0.7 copy-done.4
  2.1 0.0 copy-start.7
  2.1 0.0 copy-start.1
  2.1 0.0 copy-start.3
  2.1 0.0 copy-start.5
  2.1 1.7 %roll.1 = (f32[32,64,128]{2,1,0:T(8,128)S(1)}, f32[32,32,128]{2,1,0:T(8,128)S(1)}) custom-call(s32[3]{0:T(128)S(1)} %copy-done.4, f32[3,64,2048]{2,1,0:T(8,128)S(1)} %copy-done), custom_call_target="tpu_custom_call" | custom-call | tf_op jit(solution)/shard_map/roll/pallas_call | solution.py:345
  3.8 0.0 copy-start.2
  3.8 0.6 collective-permute-start
  4.3 0.0 copy-done.7
  4.3 0.1 reshape.59
  4.4 0.6 dynamic_slice.3
  5.0 0.0 copy-done.6
  5.0 0.1 pad_add_fusion
  5.1 0.1 copy.12
  5.2 0.1 copy.13
  5.3 0.1 copy.14
  5.4 0.1 reshape.60.place_ref
  6.1 0.0 collective-permute-done
  6.2 0.1 select_dynamic-update-slice_fusion.own_ref
  6.3 0.0 copy-done.1
  6.3 0.0 copy-done.3
  6.3 0.0 copy-done.5
  6.3 26.2 %scatter.8 = (bf16[128,192]{1,0:T(8,128)(2,1)S(1)}, bf16[64,192]{1,0:T(8,128)(2,1)S(1)}, bf16[2560,256]{1,0:T(8,128)(2,1)S(1)}, bf16[1536,256]{1,0:T(8,128)(2,1)...) custom-call(f32[15]{0:T(128)S(1)} %copy-done.3, f32[16]{0:T(128)S(1)} %copy-done.5, ...), custom_call_target="tpu_custom_call" | custom-call | tf_op jit(solution)/shard_map/scatter/pallas_call | solution.py:368
  32.6 0.0 copy-done.2
  32.6 1.5 %mix.1 = (f32[2048,128]{1,0:T(8,128)S(1)}, f32[2,40,128]{2,1,0:T(8,128)S(1)}) custom-call(f32[2048,128]{1,0:T(8,128)S(1)} %bitcast.9, bf16[64,192]{1,0:T(8,128)(2,1)S(1)} %get-tuple-element.33.mix_ref, f32[32,128]{1,0:T(8,128)S(1)} %bitcast.13), custom_call_target="tpu_custom_call" | custom-call | tf_op jit(solution)/shard_map/mix/pallas_call | solution.py:386
  34.1 36.1 %give_back.1 = (f32[32,64,128]{2,1,0:T(8,128)S(1)}, f32[32,40,128]{2,1,0:T(8,128)S(1)}) custom-call(f32[32,64,128]{2,1,0:T(8,128)S(1)} %bitcast.10, f32[2,40,128]{2,1,0:T(8,128)S(1)} %get-tuple-element.35.pots_ref), custom_call_target="tpu_custom_call" | custom-call | tf_op jit(solution)/shard_map/give_back/pallas_call | solution.py:396
  70.2 11.6 %filter.1 = f32[2,64,2048]{2,1,0:T(8,128)} custom-call(f32[15]{0:T(128)S(1)} %copy-done.3, f32[2048,128]{1,0:T(8,128)S(1)} %bitcast.11, f32[1280,128]{1,0:T(8,128)S(1)} %bitcast.12, bf16[128,192]{1,0:T(8,128)(2,1)S(1)} %get-tuple-element.38.xf_ref, bf16[64,192]{1,0:T(8,128)(2,1)S(1)} %get-tuple-element.39.xb_ref, ...), custom_call_target="tpu_custom_call" | custom-call | tf_op jit(solution)/shard_map/filter/pallas_call | solution.py:408
  (2 shorter events, 0.0 us)
Async XLA Ops:
  0.0 5.0 %copy-start.6 = (s32[2]{0:T(128)S(1)}, s32[2]{0:T(128)}, u32[]{:S(2)}) copy-start(s32[2]{0:T(128)} %constant.52) | copy-start | bytes 28
  0.0 1.4 %copy-start = (f32[3,64,2048]{2,1,0:T(8,128)S(1)}, f32[3,64,2048]{2,1,0:T(8,128)}, u32[]{:S(2)}) copy-start(f32[3,64,2048]{2,1,0:T(8,128)} %slots_ref.1) | copy-start | bytes 4718596
  1.4 0.7 copy-start.4
  2.1 2.3 %copy-start.7 = (s32[32]{0:T(128)S(1)}, s32[32]{0:T(128)}, u32[]{:S(2)}) copy-start(s32[32]{0:T(128)} %param.11) | copy-start | bytes 388
  2.1 4.2 %copy-start.1 = (f32[64,64]{1,0:T(8,128)S(1)}, f32[64,64]{1,0:T(8,128)}, u32[]{:S(2)}) copy-start(f32[64,64]{1,0:T(8,128)} %kernel_ref.1) | copy-start | bytes 49156
  2.1 4.2 %copy-start.3 = (f32[15]{0:T(128)S(1)}, f32[15]{0:T(128)}, u32[]{:S(2)}) copy-start(f32[15]{0:T(128)} %kin_ref.3) | copy-start | bytes 184
  2.1 4.2 %copy-start.5 = (f32[16]{0:T(128)S(1)}, f32[16]{0:T(128)}, u32[]{:S(2)}) copy-start(f32[16]{0:T(128)} %mag_ref.1) | copy-start | bytes 196
  3.8 28.8 %copy-start.2 = (f32[4096]{0:T(1024)S(1)}, f32[4096]{0:T(1024)}, u32[]{:S(2)}) copy-start(f32[4096]{0:T(1024)} %param.14) | copy-start | bytes 49156
  3.8 2.4 %collective-permute-start = (f32[32,32,128]{2,1,0:T(8,128)S(1)}, f32[32,32,128]{2,1,0:T(8,128)S(1)}, u32[]{:S(2)}, u32[]{:S(2)}) collective-permute-start(f32[32,32,128]{2,1,0:T(8,128)S(1)} %get-tuple-element.31), channel_id=1, source_target_pairs={{0,1},{1,0},{2,3},{3,2},{4,5},{5,4},{6,7},{7,6},{8,9},{9,8},{10,11... | collective-permute-start | bytes 1572872 | tf_op jit(solution)/shard_map/ppermute | solution.py:356

commit v2 on v1

--- a/solution.py
+++ b/solution.py
@@ -12,6 +12,7 @@
 LANES = 128
 SLAB = 256
 YS = SLAB // NZ
+GROUP = 4
 VMEM = pl.BlockSpec(memory_space=pltpu.VMEM)
 SMEM = pl.BlockSpec(memory_space=pltpu.SMEM)
 F32 = jnp.float32
@@ -182,33 +183,57 @@
         copy.wait()
 
 
-def return_kernel(devices, mixed_ref, pots_ref, got_ref, gpot_ref, send_sem, recv_sem, own_send, own_recv, relay_send, relay_recv):
+def return_kernel(devices, mixed_ref, pots_ref, got_ref, gpot_ref, send_sem, recv_sem, own_send, own_recv,
+                  relay_send, relay_recv, core_send, core_recv):
     me = lax.axis_index("fn")
     half = devices // 2
     side = me // half
     across = partner(me, half)
+    other_core = partner(me, 1)
     greet(me, devices)
+
+    def to_core(source, owner, k):
+        copy = remote(source, gpot_ref.at[owner], core_send.at[k], core_recv.at[k], other_core)
+        copy.start()
+        return copy
+
     handed = remote(pots_ref.at[1 - side], gpot_ref.at[me], own_send.at[0], own_recv.at[0], across)
     handed.start()
-    copies = []
-    for k in range(1, half):
-        copy = remote(pots_ref.at[side], gpot_ref.at[me], own_send.at[k], own_recv.at[k], partner(me, k))
-        copy.start()
-        copies.append(copy)
+    direct, relays, blocks, core = {}, {}, [], []
+    for k in range(2, half, 2):
+        direct[k] = remote(pots_ref.at[side], gpot_ref.at[me], own_send.at[k], own_recv.at[k], partner(me, k))
+        direct[k].start()
+    core.append(to_core(pots_ref.at[side], me, 0))
+
+    def give(ks):
+        for k in ks:
+            there = partner(me, k)
+            copy = remote(mixed_ref.at[there], got_ref.at[me], send_sem.at[k], recv_sem.at[k], there)
+            copy.start()
+            blocks.append(copy)
+
     order = far_first(devices)
-    for n, k in enumerate(order):
-        there = partner(me, k)
-        copy = remote(mixed_ref.at[there], got_ref.at[me], send_sem.at[k], recv_sem.at[k], there)
-        copy.start()
-        copies.append(copy)
+    ahead = len(order) // 3
+    give(order[:ahead])
+    handed.wait()
+    for k in range(2, half, 2):
+        relays[k] = remote(gpot_ref.at[across], gpot_ref.at[across], relay_send.at[k], relay_recv.at[k], partner(me, k))
+        relays[k].start()
+    core.append(to_core(gpot_ref.at[across], across, half))
+    give(order[ahead:])
     got_ref[me] = mixed_ref[me]
     gpot_ref[me] = pots_ref[side]
-    handed.wait()
-    for k in range(1, half):
-        copy = remote(gpot_ref.at[across], gpot_ref.at[across], relay_send.at[k], relay_recv.at[k], partner(me, k))
-        copy.start()
-        copies.append(copy)
-    for copy in copies:
+    for k, copy in direct.items():
+        copy.wait_recv()
+        owner = partner(me, k)
+        core.append(to_core(gpot_ref.at[owner], owner, k))
+    for k, copy in relays.items():
+        copy.wait_recv()
+        owner = partner(me, k + half)
+        core.append(to_core(gpot_ref.at[owner], owner, k + half))
+    for copy in [*direct.values(), *relays.values()]:
+        copy.wait_send()
+    for copy in blocks + core:
         copy.wait()
 
 
@@ -287,22 +312,32 @@
     def banded(hi_ref, lo_ref, matrix_ref, h):
         width = matrix_ref.shape[0] // 2
         count = width // SLAB
-        places = [lax.rem(h + (n - count // 2) + slabs, slabs) for n in range(count)]
-        high = jnp.concatenate([hi_ref[place] for place in places], axis=1)
-        low = jnp.concatenate([lo_ref[place] for place in places], axis=1)
+
+        def wide(ref):
+            return jnp.concatenate([
+                jnp.concatenate(
+                    [ref[lax.rem(h + g + (n - count // 2) + slabs, slabs)] for n in range(count)], axis=1
+                ) for g in range(GROUP)
+            ], axis=0)
+
+        high, low = wide(hi_ref), wide(lo_ref)
         return dot(high, matrix_ref[:width]) + (dot(low, matrix_ref[:width]) + dot(high, matrix_ref[width:]))
 
-    def forward(h, carry):
-        acc_ref[h] += banded(v_hi, v_lo, kinm_ref, h)
+    def forward(step, carry):
+        h = step * GROUP
+        kinetic = banded(v_hi, v_lo, kinm_ref, h)
         smooth = banded(p_hi, p_lo, fwd_ref, h)
-        potential = pot_ref[h]
-        for f in range(local):
-            high, low = halves(smooth[f * nx:(f + 1) * nx] * potential)
-            mixed = dot(xb_ref[...], jnp.concatenate([high, high, low], axis=0))
-            w_hi[h, f * nx:(f + 1) * nx], w_lo[h, f * nx:(f + 1) * nx] = halves(mixed)
+        for g in range(GROUP):
+            base = g * local * nx
+            acc_ref[h + g] += kinetic[base:base + local * nx]
+            potential = pot_ref[h + g]
+            for f in range(local):
+                high, low = halves(smooth[base + f * nx:base + (f + 1) * nx] * potential)
+                mixed = dot(xb_ref[...], jnp.concatenate([high, high, low], axis=0))
+                w_hi[h + g, f * nx:(f + 1) * nx], w_lo[h + g, f * nx:(f + 1) * nx] = halves(mixed)
         return carry
 
-    lax.fori_loop(0, slabs, forward, 0)
+    lax.fori_loop(0, slabs // GROUP, forward, 0)
 
     sides = jnp.abs(kin_ref[0])
     for t in range(1, kin_ref.shape[0]):
@@ -311,21 +346,27 @@
     bound = 1.0 + 1.5 * sides + jnp.max(peaks, axis=0, keepdims=True)
     bound = jnp.concatenate([bound] * per_slab, axis=1)
 
-    def backward(h, carry):
-        result = (acc_ref[h] + banded(w_hi, w_lo, bwd_ref, h)) / bound
-        lanes = pl.multiple_of(h * SLAB, SLAB)
-        for f in range(local):
-            for xo in range(spread):
-                count = nx // spread
-                block = result[f * nx + xo * count:f * nx + (xo + 1) * count]
+    def backward(step, carry):
+        first = step * GROUP
+        back = banded(w_hi, w_lo, bwd_ref, first)
+        count = nx // spread
+        for g in range(GROUP):
+            h = first + g
+            result = (acc_ref[h] + back[g * local * nx:(g + 1) * local * nx]) / bound
+            for f in range(local):
                 for k in range(per_slab):
-                    stage_ref[f, h * per_slab + k, pl.ds(xo, count, stride=spread), :] = block[:, k * LANES:(k + 1) * LANES]
-        for f in range(local):
-            for k in range(per_slab):
-                out_ref[f, :, pl.ds(pl.multiple_of(lanes + k * LANES, LANES), LANES)] = stage_ref[f, h * per_slab + k]
+                    q = h * per_slab + k
+                    if spread > 1:
+                        for xo in range(spread):
+                            block = result[f * nx + xo * count:f * nx + (xo + 1) * count, k * LANES:(k + 1) * LANES]
+                            stage_ref[f, q, pl.ds(xo, count, stride=spread), :] = block
+                        ordered = stage_ref[f, q]
+                    else:
+                        ordered = result[f * nx:(f + 1) * nx, k * LANES:(k + 1) * LANES]
+                    out_ref[f, :, pl.ds(pl.multiple_of(q * LANES, LANES), LANES)] = ordered
         return carry
 
-    lax.fori_loop(0, slabs, backward, 0)
+    lax.fori_loop(0, slabs // GROUP, backward, 0)
 
 
 def shaped(shape, dtype=F32):
@@ -398,7 +439,7 @@
         out_shape=(shaped((devices, local * rows_per, LANES)), shaped((devices, rows_per + 8, LANES))),
         in_specs=[VMEM, VMEM],
         out_specs=(VMEM, VMEM),
-        scratch_shapes=[each] * 6,
+        scratch_shapes=[each] * 8,
         compiler_params=params(collective_id=1),
         name="give_back",
     )(mixed.reshape(devices, local * rows_per, LANES), pots)

time: 81.9 us -> 76.5 us (0.934)
  Pallas kernels: 77.1 us -> 71 us
    pallas_call x1, Pallas kernels: 11.6 us -> 8.12 us  [body(): pl.pallas_call(functools.partial(filter_kernel, devices, rows_per), out_s...]
    pallas_call x1, Pallas kernels: 36.1 us -> 33.5 us  [body(): pl.pallas_call(functools.partial(return_kernel, devices), out_shape=(shap...]
where the time goes in v2:
time: 76.5 us; the launch traced here: 75.7 us
  Pallas kernels  71 us (93%)
  local copies, waits for them, and re-layouts  3.15 us (4%)
    pallas_call x1, Pallas kernels, body(): pl.pallas_call(functools.partial(return_kernel, devices), out_shape=(shap...  33.5 us
    pallas_call x1, Pallas kernels, body(): pl.pallas_call(functools.partial(scatter_kernel, devices), out_shape=(sha...  26.2 us
    pallas_call x1, Pallas kernels, body(): pl.pallas_call(functools.partial(filter_kernel, devices, rows_per), out_s...  8.12 us
    unnamed x16, local copies, waits for them, and re-layouts  2.1 us
    pallas_call x1, Pallas kernels, body(): pl.pallas_call(functools.partial(roll_kernel, rows_per), out_shape=(shape...  1.67 us
  transfers between devices with their start and end apart: 1, of which 0 were waited for; matrix products, arithmetic and copies ran while one was open for 1% of the time, Pallas kernels for 0%

profile of v2, /device:TPU:0, one launch (start us, length us, event | category | flops | bytes accessed | tf_op | source)
XLA Modules:
  0.0 75.7 jit_solution(6734924137506342707)
XLA Ops:
  0.0 0.0 copy-start.6
  0.0 0.0 copy-start
  0.0 1.4 %copy-done = f32[3,64,2048]{2,1,0:T(8,128)S(1)} copy-done((f32[3,64,2048]{2,1,0:T(8,128)S(1)}, f32[3,64,2048]{2,1,0:T(8,128)}, u32[]{:S(2)}) %copy-start) | copy-done | bytes 1572888
  1.4 0.0 copy-start.4
  1.4 0.7 copy-done.4
  2.1 0.0 copy-start.7
  2.1 0.0 copy-start.1
  2.1 0.0 copy-start.3
  2.1 0.0 copy-start.5
  2.1 1.7 %roll.1 = (f32[32,64,128]{2,1,0:T(8,128)S(1)}, f32[32,32,128]{2,1,0:T(8,128)S(1)}) custom-call(s32[3]{0:T(128)S(1)} %copy-done.4, f32[3,64,2048]{2,1,0:T(8,128)S(1)} %copy-done), custom_call_target="tpu_custom_call" | custom-call | tf_op jit(solution)/shard_map/roll/pallas_call | solution.py:386
  3.8 0.0 copy-start.2
  3.8 0.6 collective-permute-start
  4.3 0.0 copy-done.7
  4.3 0.1 reshape.59
  4.4 0.6 dynamic_slice.3
  5.0 0.0 copy-done.6
  5.0 0.1 pad_add_fusion
  5.1 0.1 copy.12
  5.2 0.1 copy.13
  5.3 0.1 copy.14
  5.4 0.1 reshape.60.place_ref
  6.1 0.0 collective-permute-done
  6.2 0.1 select_dynamic-update-slice_fusion.own_ref
  6.3 0.0 copy-done.1
  6.3 0.0 copy-done.3
  6.3 0.0 copy-done.5
  6.3 26.2 %scatter.8 = (bf16[128,192]{1,0:T(8,128)(2,1)S(1)}, bf16[64,192]{1,0:T(8,128)(2,1)S(1)}, bf16[2560,256]{1,0:T(8,128)(2,1)S(1)}, bf16[1536,256]{1,0:T(8,128)(2,1)...) custom-call(f32[15]{0:T(128)S(1)} %copy-done.3, f32[16]{0:T(128)S(1)} %copy-done.5, ...), custom_call_target="tpu_custom_call" | custom-call | tf_op jit(solution)/shard_map/scatter/pallas_call | solution.py:409
  32.6 0.0 copy-done.2
  32.6 1.5 %mix.1 = (f32[2048,128]{1,0:T(8,128)S(1)}, f32[2,40,128]{2,1,0:T(8,128)S(1)}) custom-call(f32[2048,128]{1,0:T(8,128)S(1)} %bitcast.9, bf16[64,192]{1,0:T(8,128)(2,1)S(1)} %get-tuple-element.33.mix_ref, f32[32,128]{1,0:T(8,128)S(1)} %bitcast.13), custom_call_target="tpu_custom_call" | custom-call | tf_op jit(solution)/shard_map/mix/pallas_call | solution.py:427
  34.1 33.5 %give_back.1 = (f32[32,64,128]{2,1,0:T(8,128)S(1)}, f32[32,40,128]{2,1,0:T(8,128)S(1)}) custom-call(f32[32,64,128]{2,1,0:T(8,128)S(1)} %bitcast.10, f32[2,40,128]{2,1,0:T(8,128)S(1)} %get-tuple-element.35.pots_ref), custom_call_target="tpu_custom_call" | custom-call | tf_op jit(solution)/shard_map/give_back/pallas_call | solution.py:437
  67.6 8.1 %filter.1 = f32[2,64,2048]{2,1,0:T(8,128)} custom-call(f32[15]{0:T(128)S(1)} %copy-done.3, f32[2048,128]{1,0:T(8,128)S(1)} %bitcast.11, f32[1280,128]{1,0:T(8,128)S(1)} %bitcast.12, bf16[128,192]{1,0:T(8,128)(2,1)S(1)} %get-tuple-element.38.xf_ref, bf16[64,192]{1,0:T(8,128)(2,1)S(1)} %get-tuple-element.39.xb_ref, ...), custom_call_target="tpu_custom_call" | custom-call | tf_op jit(solution)/shard_map/filter/pallas_call | solution.py:449
  (2 shorter events, 0.0 us)
Async XLA Ops:
  0.0 5.0 %copy-start.6 = (s32[2]{0:T(128)S(1)}, s32[2]{0:T(128)}, u32[]{:S(2)}) copy-start(s32[2]{0:T(128)} %constant.52) | copy-start | bytes 28
  0.0 1.4 %copy-start = (f32[3,64,2048]{2,1,0:T(8,128)S(1)}, f32[3,64,2048]{2,1,0:T(8,128)}, u32[]{:S(2)}) copy-start(f32[3,64,2048]{2,1,0:T(8,128)} %slots_ref.1) | copy-start | bytes 4718596
  1.4 0.7 copy-start.4
  2.1 2.3 %copy-start.7 = (s32[32]{0:T(128)S(1)}, s32[32]{0:T(128)}, u32[]{:S(2)}) copy-start(s32[32]{0:T(128)} %param.11) | copy-start | bytes 388
  2.1 4.2 %copy-start.1 = (f32[64,64]{1,0:T(8,128)S(1)}, f32[64,64]{1,0:T(8,128)}, u32[]{:S(2)}) copy-start(f32[64,64]{1,0:T(8,128)} %kernel_ref.1) | copy-start | bytes 49156
  2.1 4.2 %copy-start.3 = (f32[15]{0:T(128)S(1)}, f32[15]{0:T(128)}, u32[]{:S(2)}) copy-start(f32[15]{0:T(128)} %kin_ref.3) | copy-start | bytes 184
  2.1 4.2 %copy-start.5 = (f32[16]{0:T(128)S(1)}, f32[16]{0:T(128)}, u32[]{:S(2)}) copy-start(f32[16]{0:T(128)} %mag_ref.1) | copy-start | bytes 196
  3.8 28.8 %copy-start.2 = (f32[4096]{0:T(1024)S(1)}, f32[4096]{0:T(1024)}, u32[]{:S(2)}) copy-start(f32[4096]{0:T(1024)} %param.14) | copy-start | bytes 49156
  3.8 2.4 %collective-permute-start = (f32[32,32,128]{2,1,0:T(8,128)S(1)}, f32[32,32,128]{2,1,0:T(8,128)S(1)}, u32[]{:S(2)}, u32[]{:S(2)}) collective-permute-start(f32[32,32,128]{2,1,0:T(8,128)S(1)} %get-tuple-element.31), channel_id=1, source_target_pairs={{0,1},{1,0},{2,3},{3,2},{4,5},{5,4},{6,7},{7,6},{8,9},{9,8},{10,11... | collective-permute-start | bytes 1572872 | tf_op jit(solution)/shard_map/ppermute | solution.py:397
